TPU v7x, 32 devices: a whole 2x2x4 slice. The times are simulated.
32 devices in a mesh: row: 8 (over y, x, core), col: 4 (over z).
Axes of the slice: x: 2, y: 2, z: 4, core: 2. Of those that a mesh axis runs over, the one named last changes fastest.
Arguments:
- trials: float32 [2, 512, 1024], P(None, 'col', 'row'), may hold values from -6 to 6
- valence_factor: float32 [16384, 512], P('row'), may hold values from -0.25 to 0.25
- conduction_factor: float32 [16384, 1024], P('col', 'row'), may hold values from -0.046875 to 0.046875
- screened: float32 [16384, 16384], P('row', 'col'), may hold values from -6 to 6
- valence_energy: float32 [512], P('col'), may hold values from -0.6 to -0.1
- conduction_energy: float32 [1024], P('row'), may hold values from 0.1 to 0.6
Outputs:
- applied: float32 [2, 512, 1024], P(None, 'col', 'row')
All inputs are finite; a program needn't handle non-finite values.
Results may differ from a plain program's by a relative error of at most 0.0001.
Values sent between devices are 32-bit elements; how exact they have to be, the bound alone decides.
A program may use at most 256 MiB of HBM per device.

v0:
```python
import jax
import jax.numpy as jnp
from jax import lax
from jax.sharding import PartitionSpec as P


def body(trials, valence_factor, conduction_factor, screened, valence_energy, conduction_energy):
    highest = lax.Precision.HIGHEST
    all_valence = lax.all_gather(trials, "col", axis=1, tiled=True)
    partial_value = jnp.einsum("bvc,nc->bvn", all_valence, conduction_factor, precision=highest)
    points = lax.psum(partial_value, "row")
    expanded = jnp.einsum("mv,bvn->bmn", valence_factor, points, precision=highest)
    weighted = expanded * screened[None]
    folded = jnp.einsum("mv,bmn->bvn", valence_factor, weighted, precision=highest)
    shares = lax.psum_scatter(folded, "row", scatter_dimension=1, tiled=True)
    factor_full = lax.all_gather(conduction_factor, "row", axis=1, tiled=True)
    kernel_rows = jnp.einsum("bvn,nc->bvc", shares, factor_full, precision=highest)
    swapped = lax.all_to_all(kernel_rows, "row", split_axis=2, concat_axis=1, tiled=True)
    kernel_term = lax.psum_scatter(swapped, "col", scatter_dimension=1, tiled=True)
    differences = conduction_energy[None, :] - valence_energy[:, None]
    return differences[None] * trials - kernel_term


def solution(mesh):
    in_specs = (
        P(None, "col", "row"),
        P("row", None),
        P("col", "row"),
        P("row", "col"),
        P("col"),
        P("row"),
    )
    out_specs = P(None, "col", "row")
    return jax.shard_map(body, mesh=mesh, in_specs=in_specs, out_specs=out_specs, check_vma=False)
```

profile of v0, /device:TPU:0, one launch (start us, length us, event | category | flops | bytes accessed | tf_op | source)
XLA Modules:
  0.0 781.5 jit_solution(15031919599068699911)
XLA Ops:
  6.5 0.0 all-reduce.2.cloned.1.call-start
  6.5 17.6 %all_gather.6 = f32[2,512,128]{2,1,0:T(8,128)S(1)} all-gather(f32[2,128,128]{2,1,0:T(8,128)} %param.6), channel_id=1, replica_groups=mesh['row'=8,'col'=4] {'col'}, dimensions={1}, use_global_device_ids=true | all-gather | bytes 655360 | tf_op jit(solution)/shard_map/all_gather | solution.py:9
  24.1 16.8 %fusion.8 = f32[2,512,4096]{2,1,0:T(8,128)} fusion(f32[2,512,128]{2,1,0:T(8,128)S(1)} %all_gather.6, f32[4096,128]{1,0:T(8,128)} %param.8), kind=kOutput, calls=%fused_computation.9 | convolution fusion | flops 6442450944 | bytes 19398656 | tf_op jit(solution)/shard_map/bvc,nc->bvn/dot_general | solution.py:10
  40.9 0.0 all-reduce.2.cloned.1.call-update
  40.9 0.0 all-gather.2.cloned.1.call-start
  41.0 0.7 all-gather.2.cloned.1.call-update
  41.7 0.0 reduce-scatter.3.cloned.1.call-start
  41.7 33.8 %copy.9 = f32[2048,4096]{0,1:T(8,128)} copy(f32[2048,4096]{1,0:T(8,128)} %param.9) | data formatting | bytes 67108864 | tf_op args[3]
  75.5 185.1 %all-reduce.2.cloned.1.call-done = f32[2,512,4096]{2,1,0:T(8,128)} async-done(((f32[2,512,4096]{2,1,0:T(8,128)}), f32[2,512,4096]{2,1,0:T(8,128)}) %all-reduce.2.cloned.1.call-update) | async-done | bytes 16777232 | tf_op jit(solution)/shard_map/psum | solution.py:11
  260.6 0.0 copy-start
  260.6 217.2 %fusion.6 = f32[2,4096,2048]{2,1,0:T(8,128)} fusion(f32[2,512,4096]{2,1,0:T(8,128)} %all-reduce.2.cloned.1.call-done, f32[2048,512]{1,0:T(8,128)} %param.7), kind=kOutput, calls=%fused_computation.7 | convolution fusion | flops 103079215104 | bytes 88080384 | tf_op jit(solution)/shard_map/mv,bvn->bmn/dot_general | solution.py:12
  477.8 0.0 copy-done
  477.8 125.9 %fusion.4 = f32[2,512,4096]{2,1,0:T(8,128)} fusion(f32[2,4096,2048]{2,1,0:T(8,128)} %fusion.6, f32[2048,4096]{0,1:T(8,128)} %copy.9, f32[2048,512]{1,0:T(8,128)S(1)} %copy-done), kind=kOutput, calls=%fused_computation.5 | convolution fusion | flops 103095992320 | bytes 121634816 | tf_op jit(solution)/shard_map/mv,bmn->bvn/dot_general | solution.py:14
  603.7 0.0 reduce-scatter.3.cloned.1.call-update
  603.8 0.0 copy-start.2
  603.8 0.0 copy-start.3
  603.8 0.0 copy-start.1
  603.8 0.0 reduce-scatter.5.cloned.1.call-start
  603.9 0.0 all-gather.2.cloned.1.call-done
  603.9 116.3 %reduce-scatter.3.cloned.1.call-done = f32[2,64,4096]{2,1,0:T(8,128)} async-done(((f32[2,512,4096]{2,1,0:T(8,128)}), f32[2,64,4096]{2,1,0:T(8,128)}) %reduce-scatter.3.cloned.1.call-update) | async-done | bytes 2097168 | tf_op jit(solution)/shard_map/reduce_scatter | solution.py:15
  720.1 13.6 %fusion.2 = f32[2,64,1024]{2,1,0:T(8,128)S(1)} fusion(f32[2,64,4096]{2,1,0:T(8,128)} %reduce-scatter.3.cloned.1.call-done, f32[4096,1024]{1,0:T(8,128)} %all-gather.2.cloned.1.call-done), kind=kOutput, calls=%fused_computation.3 | convolution fusion | flops 6442450944 | bytes 19398656 | tf_op jit(solution)/shard_map/bvn,nc->bvc/dot_general | solution.py:17
  733.7 0.6 copy.10
  734.3 1.1 reshape.31
  735.4 12.2 %all_to_all.18 = f32[8,1,16384]{2,1,0:T(1,128)S(1)} all-to-all(f32[8,1,16384]{2,1,0:T(1,128)S(1)} %reshape.31), channel_id=1, replica_groups=mesh['row'=8,'col'=4] {'row'}, dimensions={0} | all-to-all | bytes 1048576 | tf_op jit(solution)/shard_map/all_to_all | solution.py:18
  747.6 0.5 broadcast.20
  748.1 1.9 reduce
  750.0 0.8 reshape.32
  750.8 1.2 copy.11
  752.0 0.0 reduce-scatter.5.cloned.1.call-update
  752.0 0.0 copy-done.2
  752.0 0.0 copy-done.3
  752.0 0.1 broadcast_subtract_fusion
  752.1 21.0 %reduce-scatter.5.cloned.1.call-done = f32[2,128,128]{2,1,0:T(8,128)} async-done(((f32[2,512,128]{2,1,0:T(8,128)}), f32[2,128,128]{2,1,0:T(8,128)}) %reduce-scatter.5.cloned.1.call-update) | async-done | bytes 131088 | tf_op jit(solution)/shard_map/reduce_scatter | solution.py:19
  773.1 0.0 copy-done.1
  773.1 1.6 multiply_subtract_fusion
Async XLA Ops:
  6.5 254.1 %all-reduce.2.cloned.1.call-start = ((), (), s32[]{:S(2)}) async-start(), calls=%async_computation.3 | async-start | bytes 33554432 | tf_op jit(solution)/shard_map/psum | solution.py:11
  40.9 563.0 %all-gather.2.cloned.1.call-start = ((), (), s32[]{:S(2)}) async-start(), calls=%async_computation.5 | async-start | bytes 18874368 | tf_op jit(solution)/shard_map/all_gather | solution.py:16
  41.7 678.5 %reduce-scatter.3.cloned.1.call-start = ((), (), s32[]{:S(2)}) async-start(), calls=%async_computation.4 | async-start | bytes 18874368 | tf_op jit(solution)/shard_map/reduce_scatter | solution.py:15
  260.6 217.2 %copy-start = (f32[2048,512]{1,0:T(8,128)S(1)}, f32[2048,512]{1,0:T(8,128)}, u32[]{:S(2)}) copy-start(f32[2048,512]{1,0:T(8,128)} %param.7) | copy-start | bytes 12582916
  603.8 148.2 %copy-start.2 = (f32[128]{0:T(128)S(1)}, f32[128]{0:T(128)}, u32[]{:S(2)}) copy-start(f32[128]{0:T(128)} %param.10) | copy-start | bytes 1540
  603.8 148.2 %copy-start.3 = (f32[128]{0:T(128)S(1)}, f32[128]{0:T(128)}, u32[]{:S(2)}) copy-start(f32[128]{0:T(128)} %param.11) | copy-start | bytes 1540
  603.8 169.3 %copy-start.1 = (f32[2,128,128]{2,1,0:T(8,128)S(1)}, f32[2,128,128]{2,1,0:T(8,128)}, u32[]{:S(2)}) copy-start(f32[2,128,128]{2,1,0:T(8,128)} %param.6) | copy-start | bytes 393220
  603.8 169.3 %reduce-scatter.5.cloned.1.call-start = ((), (), s32[]{:S(2)}) async-start(), calls=%async_computation.6 | async-start | bytes 655360 | tf_op jit(solution)/shard_map/reduce_scatter | solution.py:19
Sparse Core Ops, SparseCore 0:
  41.0 219.5 all-reduce.1
  262.5 93.0 all-gather.1
  603.9 116.1 reduce-scatter.2
  752.1 20.9 reduce-scatter.4
where the time goes:
time: 786 us; the launch traced here: 781 us
  matrix products  373 us (47%)
  waiting for transfers between devices  323 us (41%)
  local copies, waits for them, and re-layouts  38 us (5%)
  blocking collectives  29.8 us (4%)
  between operations  13.4 us (2%)
    dot_general x1, matrix products, body(): jnp.einsum('mv,bvn->bmn', valence_factor, points, precision=highest)  217 us
    psum x1, waiting for transfers between devices, body(): points = lax.psum(partial_value, 'row')  185 us
    dot_general x1, matrix products, body(): jnp.einsum('mv,bmn->bvn', valence_factor, weighted, precision=highest)  126 us
    reduce_scatter x1, waiting for transfers between devices, body(): shares = lax.psum_scatter(folded, 'row', scatter_dimension=1, tiled=True)  116 us
    unnamed x11, local copies, waits for them, and re-layouts  35.7 us
    reduce_scatter x1, waiting for transfers between devices, body(): lax.psum_scatter(swapped, 'col', scatter_dimension=1, tiled=True)  21 us
    all_gather x1, blocking collectives, body(): all_valence = lax.all_gather(trials, 'col', axis=1, tiled=True)  17.6 us
    dot_general x1, matrix products, body(): jnp.einsum('bvc,nc->bvn', all_valence, conduction_factor, precision=highest)  16.8 us
  transfers between devices with their start and end apart: 4, of which 3 were waited for; matrix products, arithmetic and copies ran while one was open for 48% of the time, Pallas kernels for 0%

commit v1 on v0

--- a/solution.py
+++ b/solution.py
@@ -8,7 +8,9 @@
     highest = lax.Precision.HIGHEST
     all_valence = lax.all_gather(trials, "col", axis=1, tiled=True)
     partial_value = jnp.einsum("bvc,nc->bvn", all_valence, conduction_factor, precision=highest)
-    points = lax.psum(partial_value, "row")
+    points = partial_value
+    for hop in (1, 2, 4):
+        points = points + lax.ppermute(points, "row", [(dev, dev ^ hop) for dev in range(8)])
     expanded = jnp.einsum("mv,bvn->bmn", valence_factor, points, precision=highest)
     weighted = expanded * screened[None]
     folded = jnp.einsum("mv,bmn->bvn", valence_factor, weighted, precision=highest)

time: 786 us -> 1410 us (1.79)
  waiting for transfers between devices: 323 us -> 920 us
  other arithmetic: 3.54 us -> 33.2 us
    ppermute x0 -> x3, waiting for transfers between devices: none -> 781 us  [body(): lax.ppermute(points, 'row', [(dev, dev ^ hop) for dev in range(8)])]
    psum x1 -> x0, waiting for transfers between devices: 185 us -> none  [body(): points = lax.psum(partial_value, 'row')]
    add x0 -> x2, other arithmetic: none -> 29.6 us  [body(): points + lax.ppermute(points, 'row', [(dev, dev ^ hop) for dev in range(8)])]
  transfers between devices with their start and end apart: 4 -> 6, of which waited for: 3 -> 5; matrix products, arithmetic and copies ran while one was open for 48% -> 28% of each run, Pallas kernels for 0% -> 0%
where the time goes in v1:
time: 1410 us; the launch traced here: 1400 us
  waiting for transfers between devices  920 us (65%)
  matrix products  363 us (26%)
  local copies, waits for them, and re-layouts  37.5 us (3%)
  other arithmetic  33.2 us (2%)
  blocking collectives  29.8 us (2%)
    ppermute x3, waiting for transfers between devices, body(): lax.ppermute(points, 'row', [(dev, dev ^ hop) for dev in range(8)])  781 us
    dot_general x1, matrix products, body(): jnp.einsum('mv,bvn->bmn', valence_factor, points, precision=highest)  218 us
    reduce_scatter x1, waiting for transfers between devices, body(): shares = lax.psum_scatter(folded, 'row', scatter_dimension=1, tiled=True)  118 us
    dot_general x1, matrix products, body(): jnp.einsum('mv,bmn->bvn', valence_factor, weighted, precision=highest)  116 us
    unnamed x11, local copies, waits for them, and re-layouts  35.3 us
    add x2, other arithmetic, body(): points + lax.ppermute(points, 'row', [(dev, dev ^ hop) for dev in range(8)])  29.6 us
  transfers between devices with their start and end apart: 6, of which 5 were waited for; matrix products, arithmetic and copies ran while one was open for 28% of the time, Pallas kernels for 0%

profile of v1, /device:TPU:0, one launch (start us, length us, event | category | flops | bytes accessed | tf_op | source)
XLA Modules:
  0.0 1399.9 jit_solution(5850280088801633028)
XLA Ops:
  6.5 0.0 all-gather.2.cloned.1.call-start
  6.5 17.6 %all_gather.6 = f32[2,512,128]{2,1,0:T(8,128)S(1)} all-gather(f32[2,128,128]{2,1,0:T(8,128)} %param.6), channel_id=1, replica_groups=mesh['row'=8,'col'=4] {'col'}, dimensions={1}, use_global_device_ids=true | all-gather | bytes 655360 | tf_op jit(solution)/shard_map/all_gather | solution.py:9
  24.1 15.0 %fusion.9 = f32[2,512,4096]{2,1,0:T(8,128)S(1)} fusion(f32[2,512,128]{2,1,0:T(8,128)S(1)} %all_gather.6, f32[4096,128]{1,0:T(8,128)} %param.8), kind=kOutput, calls=%fused_computation.10 | convolution fusion | flops 6442450944 | bytes 19398656 | tf_op jit(solution)/shard_map/bvc,nc->bvn/dot_general | solution.py:10
  39.1 0.1 collective-permute-start
  39.2 25.3 %collective-permute-done = f32[2,512,4096]{2,1,0:T(8,128)} collective-permute-done((f32[2,512,4096]{2,1,0:T(8,128)S(1)}, f32[2,512,4096]{2,1,0:T(8,128)}, u32[]{:S(2)}, u32[]{:S(2)}) %collective-permute-start) | collective-permute-done | bytes 16777248 | tf_op jit(solution)/shard_map/ppermute | solution.py:13
  64.5 11.8 add.13
  76.3 1.5 collective-permute-start.1
  77.8 0.0 all-gather.2.cloned.1.call-update
  77.8 0.0 reduce-scatter.3.cloned.1.call-start
  77.9 428.4 %collective-permute-done.1 = f32[2,512,4096]{2,1,0:T(8,128)} collective-permute-done((f32[2,512,4096]{2,1,0:T(8,128)}, f32[2,512,4096]{2,1,0:T(8,128)}, u32[]{:S(2)}, u32[]{:S(2)}) %collective-permute-start.1) | collective-permute-done | bytes 16777248 | tf_op jit(solution)/shard_map/ppermute | solution.py:13
  506.3 17.8 %add.14 = f32[2,512,4096]{2,1,0:T(8,128)} add(f32[2,512,4096]{2,1,0:T(8,128)} %add.13, f32[2,512,4096]{2,1,0:T(8,128)} %collective-permute-done.1) | non-fusion elementwise | flops 4194304 | bytes 50331648 | tf_op jit(solution)/shard_map/add | solution.py:13
  524.1 1.5 collective-permute-start.2
  525.6 33.4 %copy.9 = f32[2048,4096]{0,1:T(8,128)} copy(f32[2048,4096]{1,0:T(8,128)} %param.9) | data formatting | bytes 67108864 | tf_op args[3]
  559.0 0.0 copy-start
  559.0 326.8 %collective-permute-done.2 = f32[2,512,4096]{2,1,0:T(8,128)} collective-permute-done((f32[2,512,4096]{2,1,0:T(8,128)}, f32[2,512,4096]{2,1,0:T(8,128)}, u32[]{:S(2)}, u32[]{:S(2)}) %collective-permute-start.2) | collective-permute-done | bytes 16777248 | tf_op jit(solution)/shard_map/ppermute | solution.py:13
  885.8 218.3 %fusion.4 = f32[2,4096,2048]{2,1,0:T(8,128)} fusion(f32[2,512,4096]{2,1,0:T(8,128)} %add.14, f32[2,512,4096]{2,1,0:T(8,128)} %collective-permute-done.2, f32[2048,512]{1,0:T(8,128)} %param.7), kind=kOutput, calls=%fused_computation.5 | convolution fusion | flops 103083409408 | bytes 104857600 | tf_op jit(solution)/shard_map/mv,bvn->bmn/dot_general | solution.py:14
  1104.1 0.0 copy-done
  1104.1 116.3 %fusion.6 = f32[2,512,4096]{2,1,0:T(8,128)} fusion(f32[2,4096,2048]{2,1,0:T(8,128)} %fusion.4, f32[2048,4096]{0,1:T(8,128)} %copy.9, f32[2048,512]{1,0:T(8,128)S(1)} %copy-done), kind=kOutput, calls=%fused_computation.7 | convolution fusion | flops 103095992320 | bytes 121634816 | tf_op jit(solution)/shard_map/mv,bmn->bvn/dot_general | solution.py:16
  1220.4 0.0 reduce-scatter.3.cloned.1.call-update
  1220.5 0.0 copy-start.2
  1220.5 0.0 copy-start.3
  1220.5 0.0 copy-start.1
  1220.5 0.0 reduce-scatter.5.cloned.1.call-start
  1220.5 0.0 all-gather.2.cloned.1.call-done
  1220.6 118.0 %reduce-scatter.3.cloned.1.call-done = f32[2,64,4096]{2,1,0:T(8,128)} async-done(((f32[2,512,4096]{2,1,0:T(8,128)}), f32[2,64,4096]{2,1,0:T(8,128)}) %reduce-scatter.3.cloned.1.call-update) | async-done | bytes 2097168 | tf_op jit(solution)/shard_map/reduce_scatter | solution.py:17
  1338.6 13.6 fusion.2
  1352.2 0.6 copy.10
  1352.7 1.1 reshape.31
  1353.8 12.3 all_to_all.18
  1366.1 0.5 broadcast.20
  1366.6 1.9 reduce
  1368.5 0.8 reshape.32
  1369.3 1.2 copy.11
  1370.4 0.0 reduce-scatter.5.cloned.1.call-update
  1370.5 0.0 copy-done.2
  1370.5 0.0 copy-done.3
  1370.5 0.1 broadcast_subtract_fusion
  1370.6 21.0 %reduce-scatter.5.cloned.1.call-done = f32[2,128,128]{2,1,0:T(8,128)} async-done(((f32[2,512,128]{2,1,0:T(8,128)}), f32[2,128,128]{2,1,0:T(8,128)}) %reduce-scatter.5.cloned.1.call-update) | async-done | bytes 131088 | tf_op jit(solution)/shard_map/reduce_scatter | solution.py:21
  1391.6 0.0 copy-done.1
  1391.6 1.6 multiply_subtract_fusion
Async XLA Ops:
  6.5 1214.0 %all-gather.2.cloned.1.call-start = ((), (), s32[]{:S(2)}) async-start(), calls=%async_computation.4 | async-start | bytes 18874368 | tf_op jit(solution)/shard_map/all_gather | solution.py:18
  39.1 25.4 %collective-permute-start = (f32[2,512,4096]{2,1,0:T(8,128)S(1)}, f32[2,512,4096]{2,1,0:T(8,128)}, u32[]{:S(2)}, u32[]{:S(2)}) collective-permute-start(f32[2,512,4096]{2,1,0:T(8,128)S(1)} %fusion.9), channel_id=1, source_target_pairs={{0,4},{4,0},{8,12},{12,8},{16,20},{20,16},{24,28},{28,24},{1,5},{5... | collective-permute-start | bytes 50331656 | tf_op jit(solution)/shard_map/ppermute | solution.py:13
  76.3 430.0 %collective-permute-start.1 = (f32[2,512,4096]{2,1,0:T(8,128)}, f32[2,512,4096]{2,1,0:T(8,128)}, u32[]{:S(2)}, u32[]{:S(2)}) collective-permute-start(f32[2,512,4096]{2,1,0:T(8,128)} %add.13), channel_id=1, source_target_pairs={{0,8},{4,12},{8,0},{12,4},{16,24},{20,28},{24,16},{28,20},{1,9},{5... | collective-permute-start | bytes 50331656 | tf_op jit(solution)/shard_map/ppermute | solution.py:13
  77.8 1260.7 %reduce-scatter.3.cloned.1.call-start = ((), (), s32[]{:S(2)}) async-start(), calls=%async_computation.3 | async-start | bytes 18874368 | tf_op jit(solution)/shard_map/reduce_scatter | solution.py:17
  524.1 361.7 %collective-permute-start.2 = (f32[2,512,4096]{2,1,0:T(8,128)}, f32[2,512,4096]{2,1,0:T(8,128)}, u32[]{:S(2)}, u32[]{:S(2)}) collective-permute-start(f32[2,512,4096]{2,1,0:T(8,128)} %add.14), channel_id=1, source_target_pairs={{0,16},{4,20},{8,24},{12,28},{16,0},{20,4},{24,8},{28,12},{1,17},{... | collective-permute-start | bytes 50331656 | tf_op jit(solution)/shard_map/ppermute | solution.py:13
  559.0 545.1 %copy-start = (f32[2048,512]{1,0:T(8,128)S(1)}, f32[2048,512]{1,0:T(8,128)}, u32[]{:S(2)}) copy-start(f32[2048,512]{1,0:T(8,128)} %param.7) | copy-start | bytes 12582916
  1220.5 150.0 %copy-start.2 = (f32[128]{0:T(128)S(1)}, f32[128]{0:T(128)}, u32[]{:S(2)}) copy-start(f32[128]{0:T(128)} %param.10) | copy-start | bytes 1540
  1220.5 150.0 %copy-start.3 = (f32[128]{0:T(128)S(1)}, f32[128]{0:T(128)}, u32[]{:S(2)}) copy-start(f32[128]{0:T(128)} %param.11) | copy-start | bytes 1540
  1220.5 171.1 %copy-start.1 = (f32[2,128,128]{2,1,0:T(8,128)S(1)}, f32[2,128,128]{2,1,0:T(8,128)}, u32[]{:S(2)}) copy-start(f32[2,128,128]{2,1,0:T(8,128)} %param.6) | copy-start | bytes 393220
  1220.5 171.1 %reduce-scatter.5.cloned.1.call-start = ((), (), s32[]{:S(2)}) async-start(), calls=%async_computation.5 | async-start | bytes 655360 | tf_op jit(solution)/shard_map/reduce_scatter | solution.py:21
Sparse Core Ops, SparseCore 0:
  77.9 157.9 all-gather.1
  1220.6 117.9 reduce-scatter.2
  1370.6 20.9 reduce-scatter.4
